TPU v7x, 32 devices: a whole 2x2x4 slice. The times are simulated.
32 devices in a mesh: item: 8 (over z, x), bucket: 4 (over y, core).
Axes of the slice: x: 2, y: 2, z: 4, core: 2. Of those that a mesh axis runs over, the one named last changes fastest.
Arguments:
- code_rows: bfloat16 [8192, 64], P('item'), may hold values from -6 to 6
- centroids: bfloat16 [32768, 64], P('bucket'), may hold values from -0.5 to 0.5
Outputs:
- grad_codes: float32 [8192, 64], P('item')
- new_centroids: float32 [32768, 64], P('bucket')
All inputs are finite; a program needn't handle non-finite values.
Results may differ from a plain program's by a relative error of at most 0.0032.
Values sent between devices are 32-bit elements; how exact they have to be, the bound alone decides.
No kernel may reach another device: no remote copies, remote signals or barrier semaphores. Data moves between devices by JAX's collectives and lax.ppermute only.
A program may use at most 128 MiB of HBM per device.

v0:
```python
import jax
import jax.numpy as jnp
from jax import lax
from jax.sharding import PartitionSpec as P

BUCKETS = 32768
ITERS = 3
score_scale = 20.0
step_rate = 0.2
epsilon = 1e-06


def joined(value, axis, join):
    pieces = jax.tree.map(lambda part: lax.all_gather(part, axis), value)
    head = jax.tree.map(lambda part: part[0], pieces)
    tail = jax.tree.map(lambda part: part[1:], pieces)
    so_far, _ = lax.scan(lambda so_far, piece: (join(so_far, piece), None), head, tail)
    return so_far


def scores_of(code_rows, centroids):
    return score_scale * lax.dot_general(
        code_rows, centroids, (((1,), (1,)), ((), ())), preferred_element_type=jnp.float32
    )


def lse_pair(first, second):
    highest = jnp.maximum(first[0], second[0])
    return (
        highest,
        first[1] * jnp.exp(first[0] - highest) + second[1] * jnp.exp(second[0] - highest),
    )


def stats_triple(first, second):
    highest = jnp.maximum(first[0], second[0])
    return (
        highest,
        first[1] * jnp.exp(first[0] - highest) + second[1] * jnp.exp(second[0] - highest),
        first[2] + second[2],
    )


def reduce_rows(values):
    highest = jnp.max(values, axis=1)
    summed = jnp.sum(jnp.exp(values - highest[:, None]), axis=1)
    highest, summed = joined((highest, summed), "bucket", lse_pair)
    return highest + jnp.log(summed)


def reduce_cols(values):
    highest = jnp.max(values, axis=0)
    summed = jnp.sum(jnp.exp(values - highest[None, :]), axis=0)
    highest, summed = joined((highest, summed), "item", lse_pair)
    return highest + jnp.log(summed)


def rescale(own_rows, gradient):
    moved = own_rows.astype(jnp.float32) - step_rate * gradient
    return moved * lax.rsqrt(jnp.mean(moved * moved, axis=1, keepdims=True) + epsilon)


def body(code_rows, centroids):
    rows_total = code_rows.shape[0] * lax.axis_size("item")
    log_rows = jnp.log(jnp.float32(rows_total))
    log_buckets = jnp.log(jnp.float32(BUCKETS))
    potential_col = jnp.zeros((centroids.shape[0],), jnp.float32)
    potential_row = jnp.zeros((code_rows.shape[0],), jnp.float32)
    for iteration in range(ITERS):
        potential_row = -log_rows - reduce_rows(
            scores_of(code_rows, centroids) + potential_col[None, :]
        )
        potential_col = -log_buckets - reduce_cols(
            scores_of(code_rows, centroids) + potential_row[:, None]
        )
    scores = scores_of(code_rows, centroids)
    plan = jnp.exp(scores + potential_row[:, None] + potential_col[None, :] + log_rows)
    masses = jnp.sum(plan, axis=1)
    highest = jnp.max(scores, axis=1)
    totals = jnp.sum(jnp.exp(scores - highest[:, None]), axis=1)
    highest, totals, masses = joined((highest, totals, masses), "bucket", stats_triple)
    delta = (masses[:, None] * jnp.exp(scores - highest[:, None]) / totals[:, None] - plan).astype(
        jnp.bfloat16
    )
    grad_codes = lax.psum(
        score_scale * jnp.dot(delta, centroids, preferred_element_type=jnp.float32), "bucket"
    )
    local_grad = score_scale * lax.dot_general(
        delta, code_rows, (((0,), (0,)), ((), ())), preferred_element_type=jnp.float32
    )
    gradient = lax.psum(local_grad, "item")
    new_centroids = rescale(centroids, gradient)
    return (grad_codes, new_centroids)


def solution(mesh):
    return jax.shard_map(
        body,
        mesh=mesh,
        in_specs=(P("item", None), P("bucket", None)),
        out_specs=(P("item", None), P("bucket", None)),
        check_vma=False,
    )
```

profile of v0, /device:TPU:0, one launch (start us, length us, event | category | flops | bytes accessed | tf_op | source)
XLA Modules:
  0.0 586.0 jit_solution(3918211216739394180)
XLA Ops:
  8.1 14.3 %fusion.2 = (f32[1024]{0:T(1024)S(1)}, f32[1024,8192]{1,0:T(8,128)}) fusion(bf16[1024,64]{0,1:T(8,128)(2,1)S(1)} %copy-done, bf16[8192,64]{0,1:T(8,128)(2,1)} %param.17), kind=kOutput, calls=%fused_computation.49 | convolution fusion | flops 1090518016 | bytes 34738176 | tf_op jit(solution)/shard_map/dot_general | solution.py:22
  22.4 6.2 %all-gather = f32[4096]{0:T(1024)S(1)} all-gather(f32[1024]{0:T(1024)S(1)} %get-tuple-element.326), channel_id=2, replica_groups=mesh['item'=8,'bucket'=4] {'bucket'}, dimensions={0}, use_global_device_ids=true | all-gather | bytes 20480 | tf_op jit(solution)/shard_map/all_gather | solution.py:14
  28.6 13.6 %exponential_reduce_fusion.5 = f32[1024]{0:T(1024)S(1)} fusion(f32[1024,8192]{1,0:T(8,128)} %get-tuple-element.327, f32[1024]{0:T(1024)S(1)} %get-tuple-element.326), kind=kLoop, calls=%fused_computation.29 | loop fusion | flops 16776192 | bytes 33562624 | tf_op jit(solution)/shard_map/reduce_sum | solution.py:80
  47.9 12.5 %add_reduce_fusion.3 = f32[8192]{0:T(1024)S(1)} fusion(f32[1024,8192]{1,0:T(8,128)} %get-tuple-element.327, f32[1024]{0:T(1024)S(1)} %add_subtract_fusion.5), kind=kLoop, calls=%fused_computation.33 | loop fusion | flops 16769024 | bytes 33591296 | tf_op jit(solution)/shard_map/reduce_max | solution.py:52
  60.4 14.0 %exponential_reduce_fusion.4 = f32[8192]{0:T(1024)S(1)} fusion(f32[1024,8192]{1,0:T(8,128)} %get-tuple-element.327, f32[8192]{0:T(1024)S(1)} %add_reduce_fusion.3, f32[1024]{0:T(1024)S(1)} %add_subtract_fusion.5), kind=kLoop, calls=%fused_computation.28 | loop fusion | flops 25157632 | bytes 33624064 | tf_op jit(solution)/shard_map/reduce_sum | solution.py:53
  74.4 31.4 %all-gather.2 = f32[65536]{0:T(1024)S(1)} all-gather(f32[8192]{0:T(1024)S(1)} %add_reduce_fusion.3), channel_id=4, replica_groups=mesh['item'=8,'bucket'=4] {'item'}, dimensions={0}, use_global_device_ids=true | all-gather | bytes 294912 | tf_op jit(solution)/shard_map/all_gather | solution.py:14
  105.8 30.7 %all-gather.3 = f32[65536]{0:T(1024)S(1)} all-gather(f32[8192]{0:T(1024)S(1)} %exponential_reduce_fusion.4), channel_id=5, replica_groups=mesh['item'=8,'bucket'=4] {'item'}, dimensions={0}, use_global_device_ids=true | all-gather | bytes 294912 | tf_op jit(solution)/shard_map/all_gather | solution.py:14
  137.6 12.2 %add_reduce_fusion.2 = f32[1024]{0:T(1024)S(1)} fusion(f32[1024,8192]{1,0:T(8,128)} %get-tuple-element.327, f32[8192]{0:T(1024)S(1)} %add_subtract_fusion.2), kind=kLoop, calls=%fused_computation.32 | loop fusion | flops 16776192 | bytes 33591296 | tf_op jit(solution)/shard_map/reduce_max | solution.py:45
  149.8 14.3 %exponential_reduce_fusion.3 = f32[1024]{0:T(1024)S(1)} fusion(f32[1024,8192]{1,0:T(8,128)} %get-tuple-element.327, f32[1024]{0:T(1024)S(1)} %add_reduce_fusion.2, f32[8192]{0:T(1024)S(1)} %add_subtract_fusion.2), kind=kLoop, calls=%fused_computation.27 | loop fusion | flops 25164800 | bytes 33595392 | tf_op jit(solution)/shard_map/reduce_sum | solution.py:46
  174.7 12.5 %add_reduce_fusion.1 = f32[8192]{0:T(1024)S(1)} fusion(f32[1024,8192]{1,0:T(8,128)} %get-tuple-element.327, f32[1024]{0:T(1024)S(1)} %add_subtract_fusion.4), kind=kLoop, calls=%fused_computation.31 | loop fusion | flops 16769024 | bytes 33591296 | tf_op jit(solution)/shard_map/reduce_max | solution.py:52
  187.2 14.0 %exponential_reduce_fusion.2 = f32[8192]{0:T(1024)S(1)} fusion(f32[1024,8192]{1,0:T(8,128)} %get-tuple-element.327, f32[8192]{0:T(1024)S(1)} %add_reduce_fusion.1, f32[1024]{0:T(1024)S(1)} %add_subtract_fusion.4), kind=kLoop, calls=%fused_computation.26 | loop fusion | flops 25157632 | bytes 33624064 | tf_op jit(solution)/shard_map/reduce_sum | solution.py:53
  201.2 30.9 %all-gather.6 = f32[65536]{0:T(1024)S(1)} all-gather(f32[8192]{0:T(1024)S(1)} %add_reduce_fusion.1), channel_id=8, replica_groups=mesh['item'=8,'bucket'=4] {'item'}, dimensions={0}, use_global_device_ids=true | all-gather | bytes 294912 | tf_op jit(solution)/shard_map/all_gather | solution.py:14
  232.1 30.7 %all-gather.7 = f32[65536]{0:T(1024)S(1)} all-gather(f32[8192]{0:T(1024)S(1)} %exponential_reduce_fusion.2), channel_id=9, replica_groups=mesh['item'=8,'bucket'=4] {'item'}, dimensions={0}, use_global_device_ids=true | all-gather | bytes 294912 | tf_op jit(solution)/shard_map/all_gather | solution.py:14
  263.9 12.2 %add_reduce_fusion = f32[1024]{0:T(1024)S(1)} fusion(f32[1024,8192]{1,0:T(8,128)} %get-tuple-element.327, f32[8192]{0:T(1024)S(1)} %add_subtract_fusion.1), kind=kLoop, calls=%fused_computation.30 | loop fusion | flops 16776192 | bytes 33591296 | tf_op jit(solution)/shard_map/reduce_max | solution.py:45
  276.1 14.3 %exponential_reduce_fusion.1 = f32[1024]{0:T(1024)S(1)} fusion(f32[1024,8192]{1,0:T(8,128)} %get-tuple-element.327, f32[1024]{0:T(1024)S(1)} %add_reduce_fusion, f32[8192]{0:T(1024)S(1)} %add_subtract_fusion.1), kind=kLoop, calls=%fused_computation.25 | loop fusion | flops 25164800 | bytes 33595392 | tf_op jit(solution)/shard_map/reduce_sum | solution.py:46
  301.2 12.5 %add_reduce_fusion.4 = f32[8192]{0:T(1024)S(1)} fusion(f32[1024,8192]{1,0:T(8,128)} %get-tuple-element.327, f32[1024]{0:T(1024)S(1)} %add_subtract_fusion.3), kind=kLoop, calls=%fused_computation.34 | loop fusion | flops 16769024 | bytes 33591296 | tf_op jit(solution)/shard_map/reduce_max | solution.py:52
  313.7 14.0 %exponential_reduce_fusion = f32[8192]{0:T(1024)S(1)} fusion(f32[1024,8192]{1,0:T(8,128)} %get-tuple-element.327, f32[8192]{0:T(1024)S(1)} %add_reduce_fusion.4, f32[1024]{0:T(1024)S(1)} %add_subtract_fusion.3), kind=kLoop, calls=%fused_computation.24 | loop fusion | flops 25157632 | bytes 33624064 | tf_op jit(solution)/shard_map/reduce_sum | solution.py:53
  327.7 30.9 %all-gather.10 = f32[65536]{0:T(1024)S(1)} all-gather(f32[8192]{0:T(1024)S(1)} %add_reduce_fusion.4), channel_id=12, replica_groups=mesh['item'=8,'bucket'=4] {'item'}, dimensions={0}, use_global_device_ids=true | all-gather | bytes 294912 | tf_op jit(solution)/shard_map/all_gather | solution.py:14
  358.6 30.7 %all-gather.11 = f32[65536]{0:T(1024)S(1)} all-gather(f32[8192]{0:T(1024)S(1)} %exponential_reduce_fusion), channel_id=13, replica_groups=mesh['item'=8,'bucket'=4] {'item'}, dimensions={0}, use_global_device_ids=true | all-gather | bytes 294912 | tf_op jit(solution)/shard_map/all_gather | solution.py:14
  390.4 14.8 %fusion = f32[1024]{0:T(1024)S(1)} fusion(f32[1024,8192]{1,0:T(8,128)} %get-tuple-element.327, f32[8192]{0:T(1024)S(1)} %add_subtract_fusion, f32[1024]{0:T(1024)S(1)} %add_subtract_fusion.3), kind=kLoop, calls=%fused_computation.35 | loop fusion | flops 33553408 | bytes 33595392 | tf_op jit(solution)/shard_map/reduce_sum | solution.py:78
  410.7 18.8 %subtract_convert_fusion = bf16[1024,8192]{1,0:T(8,128)(2,1)S(1)} fusion(f32[1024,8192]{1,0:T(8,128)} %get-tuple-element.327, f32[1024]{0:T(1024)S(1)} %get-tuple-element.223, f32[1024]{0:T(1024)S(1)} %get-tuple-element.222, f32[1024]{0:T(1024)S(1)} %get-tuple-element.221, f32[8192]{0:T(1024)S(1)} %add_subtract_fusion, f32[1024]{0:T(1024)S(1)} %add_subtract_fusion.3), kind=kLoop, calls=%fused_computation.22 | loop fusion | flops 67108864 | bytes 50380800 | tf_op jit(solution)/shard_map/convert_element_type | solution.py:82
  439.8 11.7 %convolution_multiply_fusion.1 = f32[1024,64]{0,1:T(8,128)} fusion(bf16[1024,8192]{1,0:T(8,128)(2,1)} %copy-done.1, bf16[8192,64]{0,1:T(8,128)(2,1)S(1)} %copy-done.2), kind=kOutput, calls=%fused_computation.41 | convolution fusion | flops 1073807360 | bytes 18087936 | tf_op jit(solution)/shard_map/dot_general | solution.py:86
  451.5 91.4 %all-reduce.5.cloned.1.call-done = f32[8192,64]{0,1:T(8,128)} async-done(((f32[8192,64]{0,1:T(8,128)}), f32[8192,64]{0,1:T(8,128)}) %all-reduce.5.cloned.1.call-update) | async-done | bytes 2097168 | tf_op jit(solution)/shard_map/psum | solution.py:91
  548.2 29.2 %all-reduce.3.cloned.1.call-done = f32[1024,64]{0,1:T(8,128)} async-done(((f32[1024,64]{0,1:T(8,128)}), f32[1024,64]{0,1:T(8,128)}) %all-reduce.3.cloned.1.call-update) | async-done | bytes 262160 | tf_op jit(solution)/shard_map/psum | solution.py:85
  (147 shorter events, 56.4 us)
Async XLA Ops:
  7.2 0.9 copy-start
  7.2 535.8 %all-reduce.5.cloned.1.call-start = ((), (), s32[]{:S(2)}) async-start(), calls=%async_computation.1 | async-start | bytes 4194304 | tf_op jit(solution)/shard_map/psum | solution.py:91
  410.6 29.2 %copy-start.2 = (bf16[8192,64]{0,1:T(8,128)(2,1)S(1)}, bf16[8192,64]{0,1:T(8,128)(2,1)}, u32[]{:S(2)}) copy-start(bf16[8192,64]{0,1:T(8,128)(2,1)} %param.17) | copy-start | bytes 3145732
  429.5 5.7 copy-start.1
  439.5 137.9 %all-reduce.3.cloned.1.call-start = ((), (), s32[]{:S(2)}) async-start(), calls=%async_computation | async-start | bytes 524288 | tf_op jit(solution)/shard_map/psum | solution.py:85
Sparse Core Ops, SparseCore 0:
  439.7 103.2 all-reduce.4
  545.9 31.5 all-reduce.2
where the time goes:
time: 588 us; the launch traced here: 586 us
  blocking collectives  223 us (38%)
  other arithmetic  186 us (32%)
  waiting for transfers between devices  121 us (21%)
  matrix products  30.3 us (5%)
  between operations  14.4 us (2%)
  local copies, waits for them, and re-layouts  10.4 us (2%)
    all_gather x13, blocking collectives, joined(): pieces = jax.tree.map(lambda part: lax.all_gather(part, axis), value)  223 us
    psum x1, waiting for transfers between devices, body(): gradient = lax.psum(local_grad, 'item')  91.4 us
    reduce_sum x3, other arithmetic, reduce_cols(): summed = jnp.sum(jnp.exp(values - highest[None, :]), axis=0)  41.9 us
    reduce_max x3, other arithmetic, reduce_cols(): highest = jnp.max(values, axis=0)  37.4 us
    psum x1, waiting for transfers between devices, body(): lax.psum(score_scale * jnp.dot(delta, centroids, preferred_element_type=j...  29.2 us
    reduce_sum x2, other arithmetic, reduce_rows(): summed = jnp.sum(jnp.exp(values - highest[:, None]), axis=1)  28.6 us
    reduce_max x2, other arithmetic, reduce_rows(): highest = jnp.max(values, axis=1)  24.3 us
    convert_element_type x1, other arithmetic, body(): (masses[:, None] * jnp.exp(scores - highest[:, None]) / totals[:, None] -...  18.8 us
  transfers between devices with their start and end apart: 2, of which 2 were waited for; matrix products, arithmetic and copies ran while one was open for 3% of the time, Pallas kernels for 0%

commit v1 on v0

--- a/solution.py
+++ b/solution.py
@@ -88,7 +88,9 @@
     local_grad = score_scale * lax.dot_general(
         delta, code_rows, (((0,), (0,)), ((), ())), preferred_element_type=jnp.float32
     )
-    gradient = lax.psum(local_grad, "item")
+    gradient = local_grad
+    for hop in (1, 2, 4):
+        gradient = gradient + lax.ppermute(gradient, "item", [(dev, dev ^ hop) for dev in range(8)])
     new_centroids = rescale(centroids, gradient)
     return (grad_codes, new_centroids)
 

time: 588 us -> 636 us (1.082)
  waiting for transfers between devices: 121 us -> 177 us
  matrix products: 30.3 us -> 23.2 us
    ppermute x0 -> x3, waiting for transfers between devices: none -> 177 us  [body(): lax.ppermute(gradient, 'item', [(dev, dev ^ hop) for dev in range(8)])]
    psum x1 -> x0, waiting for transfers between devices: 91.4 us -> none  [body(): gradient = lax.psum(local_grad, 'item')]
    psum x1, waiting for transfers between devices: 29.2 us -> 0.01 us  [body(): lax.psum(score_scale * jnp.dot(delta, centroids, preferred_element_type=j...]
  transfers between devices with their start and end apart: 2 -> 4, of which waited for: 2 -> 3; matrix products, arithmetic and copies ran while one was open for 3% -> 2% of each run, Pallas kernels for 0% -> 0%
where the time goes in v1:
time: 636 us; the launch traced here: 634 us
  blocking collectives  223 us (35%)
  other arithmetic  187 us (29%)
  waiting for transfers between devices  177 us (28%)
  matrix products  23.2 us (4%)
  between operations  14.4 us (2%)
    all_gather x13, blocking collectives, joined(): pieces = jax.tree.map(lambda part: lax.all_gather(part, axis), value)  223 us
    ppermute x3, waiting for transfers between devices, body(): lax.ppermute(gradient, 'item', [(dev, dev ^ hop) for dev in range(8)])  177 us
    reduce_sum x3, other arithmetic, reduce_cols(): summed = jnp.sum(jnp.exp(values - highest[None, :]), axis=0)  41.9 us
    reduce_max x3, other arithmetic, reduce_cols(): highest = jnp.max(values, axis=0)  37.4 us
    reduce_sum x2, other arithmetic, reduce_rows(): summed = jnp.sum(jnp.exp(values - highest[:, None]), axis=1)  28.6 us
    reduce_max x2, other arithmetic, reduce_rows(): highest = jnp.max(values, axis=1)  24.3 us
    convert_element_type x1, other arithmetic, body(): (masses[:, None] * jnp.exp(scores - highest[:, None]) / totals[:, None] -...  18.8 us
    reduce_sum x1, other arithmetic, body(): masses = jnp.sum(plan, axis=1)  14.8 us
  transfers between devices with their start and end apart: 4, of which 3 were waited for; matrix products, arithmetic and copies ran while one was open for 2% of the time, Pallas kernels for 0%

profile of v1, /device:TPU:0, one launch (start us, length us, event | category | flops | bytes accessed | tf_op | source)
XLA Modules:
  0.0 634.4 jit_solution(14887621685138847062)
XLA Ops:
  8.1 14.3 %fusion.1 = (f32[1024]{0:T(1024)S(1)}, f32[1024,8192]{1,0:T(8,128)}) fusion(bf16[1024,64]{0,1:T(8,128)(2,1)S(1)} %copy-done, bf16[8192,64]{0,1:T(8,128)(2,1)} %param.17), kind=kOutput, calls=%fused_computation.49 | convolution fusion | flops 1090518016 | bytes 34738176 | tf_op jit(solution)/shard_map/dot_general | solution.py:22
  22.4 6.2 all-gather
  28.6 13.6 %exponential_reduce_fusion.5 = f32[1024]{0:T(1024)S(1)} fusion(f32[1024,8192]{1,0:T(8,128)} %get-tuple-element.327, f32[1024]{0:T(1024)S(1)} %get-tuple-element.326), kind=kLoop, calls=%fused_computation.29 | loop fusion | flops 16776192 | bytes 33562624 | tf_op jit(solution)/shard_map/reduce_sum | solution.py:80
  47.9 12.5 %add_reduce_fusion.3 = f32[8192]{0:T(1024)S(1)} fusion(f32[1024,8192]{1,0:T(8,128)} %get-tuple-element.327, f32[1024]{0:T(1024)S(1)} %add_subtract_fusion.5), kind=kLoop, calls=%fused_computation.33 | loop fusion | flops 16769024 | bytes 33591296 | tf_op jit(solution)/shard_map/reduce_max | solution.py:52
  60.4 14.0 %exponential_reduce_fusion.4 = f32[8192]{0:T(1024)S(1)} fusion(f32[1024,8192]{1,0:T(8,128)} %get-tuple-element.327, f32[8192]{0:T(1024)S(1)} %add_reduce_fusion.3, f32[1024]{0:T(1024)S(1)} %add_subtract_fusion.5), kind=kLoop, calls=%fused_computation.28 | loop fusion | flops 25157632 | bytes 33624064 | tf_op jit(solution)/shard_map/reduce_sum | solution.py:53
  74.4 31.4 %all-gather.2 = f32[65536]{0:T(1024)S(1)} all-gather(f32[8192]{0:T(1024)S(1)} %add_reduce_fusion.3), channel_id=4, replica_groups=mesh['item'=8,'bucket'=4] {'item'}, dimensions={0}, use_global_device_ids=true | all-gather | bytes 294912 | tf_op jit(solution)/shard_map/all_gather | solution.py:14
  105.8 30.7 %all-gather.3 = f32[65536]{0:T(1024)S(1)} all-gather(f32[8192]{0:T(1024)S(1)} %exponential_reduce_fusion.4), channel_id=5, replica_groups=mesh['item'=8,'bucket'=4] {'item'}, dimensions={0}, use_global_device_ids=true | all-gather | bytes 294912 | tf_op jit(solution)/shard_map/all_gather | solution.py:14
  137.6 12.2 %add_reduce_fusion.2 = f32[1024]{0:T(1024)S(1)} fusion(f32[1024,8192]{1,0:T(8,128)} %get-tuple-element.327, f32[8192]{0:T(1024)S(1)} %add_subtract_fusion.2), kind=kLoop, calls=%fused_computation.32 | loop fusion | flops 16776192 | bytes 33591296 | tf_op jit(solution)/shard_map/reduce_max | solution.py:45
  149.8 14.3 %exponential_reduce_fusion.3 = f32[1024]{0:T(1024)S(1)} fusion(f32[1024,8192]{1,0:T(8,128)} %get-tuple-element.327, f32[1024]{0:T(1024)S(1)} %add_reduce_fusion.2, f32[8192]{0:T(1024)S(1)} %add_subtract_fusion.2), kind=kLoop, calls=%fused_computation.27 | loop fusion | flops 25164800 | bytes 33595392 | tf_op jit(solution)/shard_map/reduce_sum | solution.py:46
  174.7 12.5 %add_reduce_fusion.1 = f32[8192]{0:T(1024)S(1)} fusion(f32[1024,8192]{1,0:T(8,128)} %get-tuple-element.327, f32[1024]{0:T(1024)S(1)} %add_subtract_fusion.4), kind=kLoop, calls=%fused_computation.31 | loop fusion | flops 16769024 | bytes 33591296 | tf_op jit(solution)/shard_map/reduce_max | solution.py:52
  187.2 14.0 %exponential_reduce_fusion.2 = f32[8192]{0:T(1024)S(1)} fusion(f32[1024,8192]{1,0:T(8,128)} %get-tuple-element.327, f32[8192]{0:T(1024)S(1)} %add_reduce_fusion.1, f32[1024]{0:T(1024)S(1)} %add_subtract_fusion.4), kind=kLoop, calls=%fused_computation.26 | loop fusion | flops 25157632 | bytes 33624064 | tf_op jit(solution)/shard_map/reduce_sum | solution.py:53
  201.2 30.9 %all-gather.6 = f32[65536]{0:T(1024)S(1)} all-gather(f32[8192]{0:T(1024)S(1)} %add_reduce_fusion.1), channel_id=8, replica_groups=mesh['item'=8,'bucket'=4] {'item'}, dimensions={0}, use_global_device_ids=true | all-gather | bytes 294912 | tf_op jit(solution)/shard_map/all_gather | solution.py:14
  232.1 30.7 %all-gather.7 = f32[65536]{0:T(1024)S(1)} all-gather(f32[8192]{0:T(1024)S(1)} %exponential_reduce_fusion.2), channel_id=9, replica_groups=mesh['item'=8,'bucket'=4] {'item'}, dimensions={0}, use_global_device_ids=true | all-gather | bytes 294912 | tf_op jit(solution)/shard_map/all_gather | solution.py:14
  263.9 12.2 %add_reduce_fusion = f32[1024]{0:T(1024)S(1)} fusion(f32[1024,8192]{1,0:T(8,128)} %get-tuple-element.327, f32[8192]{0:T(1024)S(1)} %add_subtract_fusion.1), kind=kLoop, calls=%fused_computation.30 | loop fusion | flops 16776192 | bytes 33591296 | tf_op jit(solution)/shard_map/reduce_max | solution.py:45
  276.1 14.3 %exponential_reduce_fusion.1 = f32[1024]{0:T(1024)S(1)} fusion(f32[1024,8192]{1,0:T(8,128)} %get-tuple-element.327, f32[1024]{0:T(1024)S(1)} %add_reduce_fusion, f32[8192]{0:T(1024)S(1)} %add_subtract_fusion.1), kind=kLoop, calls=%fused_computation.25 | loop fusion | flops 25164800 | bytes 33595392 | tf_op jit(solution)/shard_map/reduce_sum | solution.py:46
  301.2 12.5 %add_reduce_fusion.4 = f32[8192]{0:T(1024)S(1)} fusion(f32[1024,8192]{1,0:T(8,128)} %get-tuple-element.327, f32[1024]{0:T(1024)S(1)} %add_subtract_fusion.3), kind=kLoop, calls=%fused_computation.34 | loop fusion | flops 16769024 | bytes 33591296 | tf_op jit(solution)/shard_map/reduce_max | solution.py:52
  313.7 14.0 %exponential_reduce_fusion = f32[8192]{0:T(1024)S(1)} fusion(f32[1024,8192]{1,0:T(8,128)} %get-tuple-element.327, f32[8192]{0:T(1024)S(1)} %add_reduce_fusion.4, f32[1024]{0:T(1024)S(1)} %add_subtract_fusion.3), kind=kLoop, calls=%fused_computation.24 | loop fusion | flops 25157632 | bytes 33624064 | tf_op jit(solution)/shard_map/reduce_sum | solution.py:53
  327.7 30.9 %all-gather.10 = f32[65536]{0:T(1024)S(1)} all-gather(f32[8192]{0:T(1024)S(1)} %add_reduce_fusion.4), channel_id=12, replica_groups=mesh['item'=8,'bucket'=4] {'item'}, dimensions={0}, use_global_device_ids=true | all-gather | bytes 294912 | tf_op jit(solution)/shard_map/all_gather | solution.py:14
  358.6 30.7 %all-gather.11 = f32[65536]{0:T(1024)S(1)} all-gather(f32[8192]{0:T(1024)S(1)} %exponential_reduce_fusion), channel_id=13, replica_groups=mesh['item'=8,'bucket'=4] {'item'}, dimensions={0}, use_global_device_ids=true | all-gather | bytes 294912 | tf_op jit(solution)/shard_map/all_gather | solution.py:14
  390.4 14.8 %fusion = f32[1024]{0:T(1024)S(1)} fusion(f32[1024,8192]{1,0:T(8,128)} %get-tuple-element.327, f32[8192]{0:T(1024)S(1)} %add_subtract_fusion, f32[1024]{0:T(1024)S(1)} %add_subtract_fusion.3), kind=kLoop, calls=%fused_computation.35 | loop fusion | flops 33553408 | bytes 33595392 | tf_op jit(solution)/shard_map/reduce_sum | solution.py:78
  410.7 18.8 %subtract_convert_fusion = bf16[1024,8192]{1,0:T(8,128)(2,1)S(1)} fusion(f32[1024,8192]{1,0:T(8,128)} %get-tuple-element.327, f32[1024]{0:T(1024)S(1)} %get-tuple-element.223, f32[1024]{0:T(1024)S(1)} %get-tuple-element.222, f32[1024]{0:T(1024)S(1)} %get-tuple-element.221, f32[8192]{0:T(1024)S(1)} %add_subtract_fusion, f32[1024]{0:T(1024)S(1)} %add_subtract_fusion.3), kind=kLoop, calls=%fused_computation.22 | loop fusion | flops 67108864 | bytes 50380800 | tf_op jit(solution)/shard_map/convert_element_type | solution.py:82
  434.1 46.4 %collective-permute-done = f32[8192,64]{0,1:T(8,128)S(1)} collective-permute-done((f32[8192,64]{0,1:T(8,128)S(1)}, f32[8192,64]{0,1:T(8,128)S(1)}, u32[]{:S(2)}, u32[]{:S(2)}) %collective-permute-start) | collective-permute-done | bytes 2097184 | tf_op jit(solution)/shard_map/ppermute | solution.py:93
  480.7 47.0 %collective-permute-done.1 = f32[8192,64]{0,1:T(8,128)S(1)} collective-permute-done((f32[8192,64]{0,1:T(8,128)S(1)}, f32[8192,64]{0,1:T(8,128)S(1)}, u32[]{:S(2)}, u32[]{:S(2)}) %collective-permute-start.1) | collective-permute-done | bytes 2097184 | tf_op jit(solution)/shard_map/ppermute | solution.py:93
  536.1 84.1 %collective-permute-done.2 = f32[8192,64]{0,1:T(8,128)} collective-permute-done((f32[8192,64]{0,1:T(8,128)S(1)}, f32[8192,64]{0,1:T(8,128)}, u32[]{:S(2)}, u32[]{:S(2)}) %collective-permute-start.2) | collective-permute-done | bytes 2097184 | tf_op jit(solution)/shard_map/ppermute | solution.py:93
  (150 shorter events, 59.7 us)
Async XLA Ops:
  7.2 0.9 copy-start
  7.2 618.7 %all-reduce.2.cloned.1.call-start = ((), (), s32[]{:S(2)}) async-start(), calls=%async_computation | async-start | bytes 524288 | tf_op jit(solution)/shard_map/psum | solution.py:85
  410.6 119.5 %copy-start.1 = (bf16[8192,64]{0,1:T(8,128)(2,1)S(1)}, bf16[8192,64]{0,1:T(8,128)(2,1)}, u32[]{:S(2)}) copy-start(bf16[8192,64]{0,1:T(8,128)(2,1)} %param.17) | copy-start | bytes 3145732
  432.5 47.9 %collective-permute-start = (f32[8192,64]{0,1:T(8,128)S(1)}, f32[8192,64]{0,1:T(8,128)S(1)}, u32[]{:S(2)}, u32[]{:S(2)}) collective-permute-start(f32[8192,64]{0,1:T(8,128)S(1)} %convolution_multiply_fusion), channel_id=1, source_target_pairs={{0,4},{4,0},{8,12},{12,8},{16,20},{20,16},{24,28},{28,24},{1,5},{5... | collective-permute-start | bytes 6291464 | tf_op jit(solution)/shard_map/ppermute | solution.py:93
  480.7 47.1 %collective-permute-start.1 = (f32[8192,64]{0,1:T(8,128)S(1)}, f32[8192,64]{0,1:T(8,128)S(1)}, u32[]{:S(2)}, u32[]{:S(2)}) collective-permute-start(f32[8192,64]{0,1:T(8,128)S(1)} %add.163), channel_id=1, source_target_pairs={{0,8},{4,12},{8,0},{12,4},{16,24},{20,28},{24,16},{28,20},{1,9},{5... | collective-permute-start | bytes 6291464 | tf_op jit(solution)/shard_map/ppermute | solution.py:93
  528.0 92.2 %collective-permute-start.2 = (f32[8192,64]{0,1:T(8,128)S(1)}, f32[8192,64]{0,1:T(8,128)}, u32[]{:S(2)}, u32[]{:S(2)}) collective-permute-start(f32[8192,64]{0,1:T(8,128)S(1)} %add.164), channel_id=1, source_target_pairs={{0,16},{4,20},{8,24},{12,28},{16,0},{20,4},{24,8},{28,12},{1,17},{... | collective-permute-start | bytes 6291464 | tf_op jit(solution)/shard_map/ppermute | solution.py:93
Sparse Core Ops, SparseCore 0:
  536.2 31.6 all-reduce.1
